TPU v7x, 32 devices: a whole 2x2x4 slice. The times are simulated.
32 devices in a mesh: seq: 8 (over z, y), mp: 4 (over x, core).
Axes of the slice: x: 2, y: 2, z: 4, core: 2. Of those that a mesh axis runs over, the one named last changes fastest.
Arguments:
- incoming_image_patches: bfloat16 [1, 128, 128, 1152], P(None, 'seq', 'mp'), may hold values from -6 to 6
- initial_standardize_scaling: float32 [1152], replicated, may hold values from 0.1 to 1.9
- acceptance_matrix: bfloat16 [1152, 1024], P(None, 'mp'), may hold values from -0.1875 to 0.1875
- addressing_matrix: bfloat16 [1152, 1024], P(None, 'mp'), may hold values from -0.1875 to 0.1875
- content_matrix: bfloat16 [1152, 1024], P(None, 'mp'), may hold values from -0.1875 to 0.1875
- forgetting_lowdim_left_factor: bfloat16 [1152, 64], replicated, may hold values from -0.1875 to 0.1875
- forgetting_lowdim_right_factor: bfloat16 [64, 1024], P(None, 'mp'), may hold values from -1.5 to 1.5
- forgetting_baseline: float32 [1024], P('mp'), may hold values from -6 to 1
- self_token_reward: float32 [1024], P('mp'), may hold values from -3 to 3
- horizontal_cluster_scaling: float32 [1024], P('mp'), may hold values from 0.1 to 1.9
- vertical_cluster_scaling: float32 [1024], P('mp'), may hold values from 0.1 to 1.9
- temporal_mix_projection_matrix: bfloat16 [1024, 1152], P('mp'), may hold values from -0.1875 to 0.1875
- later_standardize_scaling: float32 [1152], replicated, may hold values from 0.1 to 1.9
- feature_mix_addressing_matrix: bfloat16 [1152, 4608], P('seq', 'mp'), may hold values from -0.1875 to 0.1875
- feature_mix_content_matrix: bfloat16 [4608, 1152], P('mp', 'seq'), may hold values from -0.09375 to 0.09375
Outputs:
- block_out: bfloat16 [1, 128, 128, 1152], P(None, 'seq', 'mp')
All inputs are finite; a program needn't handle non-finite values.
Results may differ from a plain program's by a relative error of at most 0.017.
Values may be sent and summed in bfloat16 or wider, within the bound.
A program may use at most 128 MiB of HBM per device.

v0:
```python
import jax
import jax.numpy as jnp
from jax import lax
from jax.sharding import PartitionSpec as P

SUBSPACE_SIZE = 64


def layer_norm(inputs, gain):
    values = inputs.astype(jnp.float32)
    average = jnp.mean(values, axis=-1, keepdims=True)
    centred = values - average
    spread = jnp.mean(centred * centred, axis=-1, keepdims=True)
    return (centred * lax.rsqrt(spread + 1e-05) * gain).astype(jnp.bfloat16)


def heads_first(array, nheads):
    number, length, inner_width = array.shape
    shaped = array.astype(jnp.float32).reshape(number, length, nheads, inner_width // nheads)
    return shaped.transpose(0, 2, 1, 3)


def recurrence(recept_in, keying_in, decays_in, valued_in, boost_in, gain):
    number, length, inner_width = recept_in.shape
    nheads = inner_width // SUBSPACE_SIZE
    head_size = inner_width // nheads
    blocks = length // 16
    acceptance_horizontal_lines = heads_first(recept_in, nheads)
    addressing_horizontal_lines = heads_first(keying_in, nheads)
    decays = heads_first(decays_in, nheads)
    content_horizontal_lines = heads_first(valued_in, nheads)
    boost = boost_in.reshape(nheads, 1, head_size)
    running = jnp.cumsum(decays, axis=2)
    before = running - decays
    before_blocks = before.reshape(number, nheads, blocks, 16, head_size)
    anchor = before_blocks[:, :, :, :1, :]
    queries = acceptance_horizontal_lines.reshape(number, nheads, blocks, 16, head_size) * jnp.exp(
        before_blocks - anchor
    )
    places = jnp.arange(length)
    limits = (jnp.arange(blocks) + 1) * 16
    usable = places[None, :] < limits[:, None]
    exponent = anchor - running[:, :, None, :, :]
    exponent = jnp.where(usable[None, None, :, :, None], exponent, -10000.0)
    weighted = addressing_horizontal_lines[:, :, None, :, :] * jnp.exp(exponent)
    scores = jnp.einsum("nhbqc,nhbsc->nhbqs", queries, weighted, precision=lax.Precision.HIGHEST)
    query_places = places.reshape(blocks, 16)
    earlier = places[None, None, :] < query_places[:, :, None]
    scores = jnp.where(earlier[None, None], scores, 0.0)
    current = jnp.sum(acceptance_horizontal_lines * boost * addressing_horizontal_lines, axis=-1)
    summed = jnp.einsum(
        "nhbqs,nhsc->nhbqc", scores, content_horizontal_lines, precision=lax.Precision.HIGHEST
    )
    summed = (
        summed.reshape(number, nheads, length, head_size)
        + current[..., None] * content_horizontal_lines
    )
    average = jnp.mean(summed, axis=-1, keepdims=True)
    centred = summed - average
    spread = jnp.mean(centred * centred, axis=-1, keepdims=True)
    normed = (
        (centred * lax.rsqrt(spread + 0.00064))
        .transpose(0, 2, 1, 3)
        .reshape(number, length, inner_width)
    )
    return (normed * gain).astype(jnp.bfloat16)


def lines_of_columns(array):
    images, height, columns, inner_width = array.shape
    return jnp.swapaxes(array, 1, 2).reshape(images * columns, height, inner_width)


def shards(
    incoming_image_patches,
    initial_standardize_scaling,
    acceptance_matrix,
    addressing_matrix,
    content_matrix,
    forgetting_lowdim_left_factor,
    forgetting_lowdim_right_factor,
    forgetting_baseline,
    self_token_reward,
    horizontal_cluster_scaling,
    vertical_cluster_scaling,
    temporal_mix_projection_matrix,
    later_standardize_scaling,
    feature_mix_addressing_matrix,
    feature_mix_content_matrix,
):
    images, row_count, part_cols, model_width = incoming_image_patches.shape
    whole_rows = lax.all_gather(incoming_image_patches, "mp", axis=2, tiled=True)
    full_cols = whole_rows.shape[2]
    inner_width = acceptance_matrix.shape[1]
    grid_shape = (images, row_count, full_cols, inner_width)
    xn1 = layer_norm(whole_rows, initial_standardize_scaling).reshape(-1, model_width)
    acceptance_horizontal_lines = jnp.dot(
        xn1, acceptance_matrix, preferred_element_type=jnp.float32
    ).astype(jnp.bfloat16)
    addressing_horizontal_lines = jnp.dot(
        xn1, addressing_matrix, preferred_element_type=jnp.float32
    ).astype(jnp.bfloat16)
    content_horizontal_lines = jnp.dot(
        xn1, content_matrix, preferred_element_type=jnp.float32
    ).astype(jnp.bfloat16)
    latent = jnp.tanh(
        jnp.dot(xn1, forgetting_lowdim_left_factor, preferred_element_type=jnp.float32)
    ).astype(jnp.bfloat16)
    forgetting_log_amount = (
        -0.7
        * jax.nn.sigmoid(
            forgetting_baseline
            + jnp.dot(latent, forgetting_lowdim_right_factor, preferred_element_type=jnp.float32)
        )
    ).astype(jnp.bfloat16)
    recept_grid = acceptance_horizontal_lines.reshape(grid_shape)
    keying_grid = addressing_horizontal_lines.reshape(grid_shape)
    decay_grid = forgetting_log_amount.reshape(grid_shape)
    line_shape = (images * row_count, full_cols, inner_width)
    horizontal_recurrence_result = recurrence(
        acceptance_horizontal_lines.reshape(line_shape),
        addressing_horizontal_lines.reshape(line_shape),
        forgetting_log_amount.reshape(line_shape),
        content_horizontal_lines.reshape(line_shape),
        self_token_reward,
        horizontal_cluster_scaling,
    )
    col_recept, col_keying, col_decay, col_valued = (
        lax.all_to_all(recept_grid, "seq", split_axis=2, concat_axis=1, tiled=True),
        lax.all_to_all(keying_grid, "seq", split_axis=2, concat_axis=1, tiled=True),
        lax.all_to_all(decay_grid, "seq", split_axis=2, concat_axis=1, tiled=True),
        lax.all_to_all(
            horizontal_recurrence_result.reshape(grid_shape),
            "seq",
            split_axis=2,
            concat_axis=1,
            tiled=True,
        ),
    )
    height = col_recept.shape[1]
    columns = col_recept.shape[2]
    vertical_recurrence_result = recurrence(
        lines_of_columns(col_recept),
        lines_of_columns(col_keying),
        lines_of_columns(col_decay),
        lines_of_columns(col_valued),
        self_token_reward,
        vertical_cluster_scaling,
    )
    back_grid = jnp.swapaxes(
        vertical_recurrence_result.reshape(images, columns, height, inner_width), 1, 2
    )
    row_grid = lax.all_to_all(back_grid, "seq", split_axis=1, concat_axis=2, tiled=True)
    partial_value = jnp.dot(
        row_grid.reshape(-1, inner_width),
        temporal_mix_projection_matrix,
        preferred_element_type=jnp.float32,
    )
    partial_value = lax.optimization_barrier(partial_value.astype(jnp.bfloat16)).astype(jnp.float32)
    partial_value = partial_value.reshape(images, row_count, full_cols, model_width)
    totals = lax.psum(partial_value.astype(jnp.bfloat16), "mp").astype(jnp.float32)
    residual_all = (whole_rows.astype(jnp.float32) + totals).astype(jnp.bfloat16)
    mix_input = layer_norm(residual_all, later_standardize_scaling)
    residual = lax.dynamic_slice_in_dim(
        residual_all, lax.axis_index("mp") * part_cols, part_cols, 2
    )
    flattened = mix_input.reshape(-1, model_width)
    hidden_pre = jnp.dot(
        flattened,
        lax.all_gather(feature_mix_addressing_matrix, "seq", axis=0, tiled=True),
        preferred_element_type=jnp.float32,
    )
    positive = jnp.maximum(hidden_pre, 0.0)
    hidden = (positive * positive).astype(jnp.bfloat16)
    downward = jnp.dot(
        hidden,
        lax.all_gather(feature_mix_content_matrix, "seq", axis=1, tiled=True),
        preferred_element_type=jnp.float32,
    )
    downward = lax.optimization_barrier(downward.astype(jnp.bfloat16)).astype(jnp.float32)
    downward = downward.reshape(images, row_count, full_cols, model_width)
    mixed = lax.psum_scatter(
        downward.astype(jnp.bfloat16), "mp", scatter_dimension=2, tiled=True
    ).astype(jnp.float32)
    return (residual.astype(jnp.float32) + mixed).astype(jnp.bfloat16)


def solution(mesh):
    placed = (
        P(None, "seq", "mp", None),
        P(),
        P(None, "mp"),
        P(None, "mp"),
        P(None, "mp"),
        P(),
        P(None, "mp"),
        P("mp"),
        P("mp"),
        P("mp"),
        P("mp"),
        P("mp", None),
        P(),
        P("seq", "mp"),
        P("mp", "seq"),
    )
    return jax.shard_map(
        shards, mesh=mesh, in_specs=placed, out_specs=P(None, "seq", "mp", None), check_vma=False
    )
```

profile of v0, /device:TPU:0, one launch (start us, length us, event | category | flops | bytes accessed | tf_op | source)
XLA Modules:
  0.0 550.7 jit_solution(13070111403937969308)
XLA Ops:
  9.0 40.9 %all-gather.4.cloned.1.call-done = bf16[1,16,128,1152]{3,2,1,0:T(8,128)(2,1)} async-done(((bf16[1,16,32,1152]{3,2,1,0:T(8,128)(2,1)}), bf16[1,16,128,1152]{3,2,1,0:T(8,128)(2,1)}) %all-gather.4.cloned.1.call-update) | async-done | bytes 4718608 | tf_op jit(solution)/shard_map/all_gather | solution.py:92
  49.9 3.2 convert_reduce_fusion
  57.0 2.2 copy-done.9
  60.8 3.1 reshape.301
  63.9 4.9 copy.216
  68.8 4.8 copy.187
  73.7 4.5 fusion.54
  78.1 3.1 reshape.302
  81.3 8.0 %bitcast_subtract_fusion = (f32[16,4,128,64]{3,0,1,2:T(8,128)S(1)}, f32[16,4,128,64]{3,0,1,2:T(8,128)}) fusion(f32[16,128,4,64]{3,2,1,0:T(4,128)} %reshape.302), kind=kOutput, calls=%fused_computation.42 | output fusion | flops 67108864 | bytes 6291456 | tf_op jit(solution)/shard_map/jit(cumsum)/reduce_window_sum | solution.py:33
  91.4 4.8 copy.196
  96.2 3.9 convolution_convert_fusion.3
  101.1 3.7 reshape.303
  104.8 3.5 copy.194
  108.3 5.7 %convolution_convert_fusion.2 = bf16[2048,256]{1,0:T(8,128)(2,1)} fusion(bf16[2048,1152]{1,0:T(8,128)(2,1)} %bitcast.152, bf16[1152,256]{1,0:T(8,128)(2,1)} %param.19), kind=kOutput, calls=%fused_computation.66 | convolution fusion | flops 1208483840 | bytes 6356992 | tf_op jit(solution)/shard_map/dot_general | solution.py:103
  114.1 2.3 copy.197
  117.8 22.1 %fusion.1 = f32[16,4,8,16,128]{4,3,2,1,0:T(8,128)S(1)} fusion(f32[16,4,128,64]{2,3,1,0:T(8,128)} %copy.196, f32[16,4,8,64]{3,2,1,0:T(8,128)S(1)} %copy.191, f32[16,4,128,64]{2,3,1,0:T(8,128)S(1)} %bitcast.135, pred[8,128]{1,0:T(8,128)(4,1)S(1)} %iota_compare_fusion.1, f32[16,4,8,16,64]{4,3,2,1,0:T(8,128)} %bitcast.161, f32[16,4,8,16,64]{4,0,1,3,2:T(8,128)} %bitcast.147), kind=kOutput, calls=%fused_computation.1 | convolution fusion | flops 818937856 | bytes 12715008 | tf_op jit(solution)/shard_map/nhbqc,nhbsc->nhbqs/dot_general | solution.py:46
  140.0 3.9 fusion.44
  143.8 3.2 copy.200
  147.1 2.9 fusion.57
  152.7 2.3 copy.201
  156.3 5.6 %all-to-all-start.3 = ((bf16[1,16,128,256]{3,1,0,2:T(8,128)(2,1)}), bf16[1,16,128,256]{3,1,0,2:T(8,128)(2,1)}, u32[]{:S(2)}, u32[]{:S(2)}) async-start(bf16[1,16,128,256]{3,1,0,2:T(8,128)(2,1)} %multiply_convert_fusion.1), calls=%async_computation.3 | async-start | bytes 2097152 | tf_op jit(solution)/shard_map/all_to_all | solution.py:132
  162.0 2.9 copy.173
  164.8 23.4 %all-to-all-done.3 = bf16[1,16,128,256]{3,1,0,2:T(8,128)(2,1)} async-done(((bf16[1,16,128,256]{3,1,0,2:T(8,128)(2,1)}), bf16[1,16,128,256]{3,1,0,2:T(8,128)(2,1)}, u32[]{:S(2)}, u32[]{:S(2)}) %all-to-all-start.3) | async-done | bytes 1048608 | tf_op jit(solution)/shard_map/all_to_all | solution.py:132
  188.2 4.2 all-to-all-start.1
  194.0 24.0 %all-to-all-done.1 = bf16[1,16,128,256]{3,1,0,2:T(8,128)(2,1)} async-done(((bf16[1,16,128,256]{3,1,0,2:T(8,128)(2,1)}), bf16[1,16,128,256]{3,1,0,2:T(8,128)(2,1)}, u32[]{:S(2)}, u32[]{:S(2)}) %all-to-all-start.1) | async-done | bytes 1048608 | tf_op jit(solution)/shard_map/all_to_all | solution.py:131
  218.1 3.6 all-to-all-start
  223.2 24.2 %all-to-all-done = bf16[1,16,128,256]{3,1,0,2:T(8,128)(2,1)S(1)} async-done(((bf16[1,16,128,256]{3,1,0,2:T(8,128)(2,1)}), bf16[1,16,128,256]{3,1,0,2:T(8,128)(2,1)S(1)}, u32[]{:S(2)}, u32[]{:S(2)}) %all-to-all-start) | async-done | bytes 1048608 | tf_op jit(solution)/shard_map/all_to_all | solution.py:129
  247.5 4.2 all-to-all-start.2
  260.5 4.6 copy.177
  265.1 6.1 %bitcast_subtract_fusion.1 = (f32[16,4,128,64]{3,0,1,2:T(8,128)S(1)}, f32[16,4,128,64]{3,0,1,2:T(8,128)}) fusion(f32[16,128,4,64]{3,0,2,1:T(8,128)} %copy.177), kind=kOutput, calls=%fused_computation.45 | output fusion | flops 67108864 | bytes 6291456 | tf_op jit(solution)/shard_map/jit(cumsum)/reduce_window_sum | solution.py:33
  271.2 2.0 copy-done.7
  273.4 4.7 copy.185
  282.3 2.8 copy.172
  288.5 3.0 copy.183
  291.5 22.4 %fusion.6 = f32[16,4,8,16,128]{4,3,2,1,0:T(8,128)S(1)} fusion(f32[16,4,128,64]{2,3,1,0:T(8,128)} %copy.185, f32[16,4,8,64]{3,2,1,0:T(8,128)S(1)} %copy.178, f32[16,4,128,64]{2,3,1,0:T(8,128)} %bitcast.140, pred[8,128]{1,0:T(8,128)(4,1)S(1)} %iota_compare_fusion.1, f32[16,4,8,16,64]{4,3,2,1,0:T(8,128)} %bitcast.160, f32[16,4,8,16,64]{4,0,1,3,2:T(8,128)} %bitcast.145), kind=kOutput, calls=%fused_computation.6 | convolution fusion | flops 818937856 | bytes 12715008 | tf_op jit(solution)/shard_map/nhbqc,nhbsc->nhbqs/dot_general | solution.py:46
  313.8 3.8 fusion.46
  317.6 4.2 copy.205
  321.8 3.2 fusion.80
  326.0 2.1 copy.210
  330.0 30.6 %all_to_all.69 = bf16[1,128,16,256]{3,2,0,1:T(8,128)(2,1)S(1)} all-to-all(bf16[1,128,16,256]{3,2,0,1:T(8,128)(2,1)S(1)} %fusion.68), channel_id=1, replica_groups=mesh['seq'=8,'mp'=4] {'seq'}, dimensions={1} | all-to-all | bytes 2097152 | tf_op jit(solution)/shard_map/all_to_all | solution.py:153
  360.7 3.7 convolution_convert_fusion.1
  365.7 91.0 %all-reduce.2.cloned.1.call-done = bf16[1,16,128,1152]{3,2,1,0:T(8,128)(2,1)} async-done(((bf16[1,16,128,1152]{3,2,1,0:T(8,128)(2,1)}), bf16[1,16,128,1152]{3,2,1,0:T(8,128)(2,1)}) %all-reduce.2.cloned.1.call-update) | async-done | bytes 4718608 | tf_op jit(solution)/shard_map/psum | solution.py:161
  456.6 5.3 convert_reduce_fusion.1
  464.0 3.2 fusion.21
  467.3 8.3 %all-gather.8.cloned.1.call-done = bf16[1152,1152]{0,1:T(8,128)(2,1)} async-done(((bf16[1152,144]{0,1:T(8,128)(2,1)}), bf16[1152,1152]{0,1:T(8,128)(2,1)}) %all-gather.8.cloned.1.call-update) | async-done | bytes 2654224 | tf_op jit(solution)/shard_map/all_gather | solution.py:177
  475.5 18.4 %convolution_convert_fusion = bf16[2048,1152]{1,0:T(8,128)(2,1)} fusion(bf16[1152,1152]{0,1:T(8,128)(2,1)} %all-gather.8.cloned.1.call-done, bf16[2048,1152]{1,0:T(8,128)(2,1)} %bitcast.153, bf16[1152,1152]{1,0:T(8,128)(2,1)} %all-gather.6.cloned.1.call-done), kind=kOutput, calls=%fused_computation.40 | convolution fusion | flops 10881073152 | bytes 14745600 | tf_op jit(solution)/shard_map/dot_general | solution.py:175
  493.9 46.6 %reduce-scatter.2.cloned.1.call-done = bf16[1,16,32,1152]{3,2,1,0:T(8,128)(2,1)} async-done(((bf16[1,16,128,1152]{3,2,1,0:T(8,128)(2,1)}), bf16[1,16,32,1152]{3,2,1,0:T(8,128)(2,1)}) %reduce-scatter.2.cloned.1.call-update) | async-done | bytes 1179664 | tf_op jit(solution)/shard_map/reduce_scatter | solution.py:182
  540.5 2.9 add_convert_fusion
  (111 shorter events, 41.5 us)
Async XLA Ops:
  7.4 353.3 %copy-start = (bf16[256,1152]{1,0:T(8,128)(2,1)S(1)}, bf16[256,1152]{1,0:T(8,128)(2,1)}, u32[]{:S(2)}) copy-start(bf16[256,1152]{1,0:T(8,128)(2,1)} %param.26) | copy-start | bytes 1769476
  7.4 42.5 %all-gather.4.cloned.1.call-start = ((), (), s32[]{:S(2)}) async-start(), calls=%async_computation.6 | async-start | bytes 5898240 | tf_op jit(solution)/shard_map/all_gather | solution.py:92
  9.0 46.1 %copy-start.17 = (f32[1152]{0:T(1024)S(1)}, f32[1152]{0:T(1024)}, u32[]{:S(2)}) copy-start(f32[1152]{0:T(1024)} %param.16) | copy-start | bytes 13828
  49.9 3.8 copy-start.1
  55.1 4.1 copy-start.21
  57.0 2.2 copy-start.9
  60.8 8.0 %copy-start.10 = (bf16[2048,256]{1,0:T(8,128)(2,1)}, bf16[2048,256]{1,0:T(8,128)(2,1)S(1)}, u32[]{:S(2)}) copy-start(bf16[2048,256]{1,0:T(8,128)(2,1)S(1)} %convolution_convert_fusion.4) | copy-start | bytes 3145732
  68.8 4.8 copy-start.23
  68.8 4.8 copy-start.24
  68.8 4.8 copy-start.25
  78.1 11.1 %copy-start.14 = (bf16[2048,256]{1,0:T(8,128)(2,1)}, bf16[2048,256]{1,0:T(8,128)(2,1)S(1)}, u32[]{:S(2)}) copy-start(bf16[2048,256]{1,0:T(8,128)(2,1)S(1)} %fusion.54) | copy-start | bytes 3145732
  89.3 1.9 copy-start.8
  89.3 7.0 %copy-start.22 = (bf16[1152,256]{1,0:T(8,128)(2,1)S(1)}, bf16[1152,256]{1,0:T(8,128)(2,1)}, u32[]{:S(2)}) copy-start(bf16[1152,256]{1,0:T(8,128)(2,1)} %param.18) | copy-start | bytes 1769476
  100.1 1.0 copy-start.12
  108.3 9.5 %copy-start.6 = (f32[16,128,4,64]{1,3,2,0:T(8,128)}, f32[16,128,4,64]{1,3,2,0:T(8,128)S(1)}, u32[]{:S(2)}) copy-start(f32[16,128,4,64]{1,3,2,0:T(8,128)S(1)} %copy.194) | copy-start | bytes 6291460
  117.8 22.1 %copy-start.3 = (bf16[32,8,16,128]{3,2,1,0:T(8,128)(2,1)}, bf16[32,8,16,128]{3,2,1,0:T(8,128)(2,1)S(1)}, u32[]{:S(2)}) copy-start(bf16[32,8,16,128]{3,2,1,0:T(8,128)(2,1)S(1)} %copy.223) | copy-start | bytes 3145732
  147.1 2.9 copy-start.4
  150.9 4.2 copy-start.19
  156.3 36.2 %copy-start.11 = (bf16[2048,256]{1,0:T(8,128)(2,1)S(1)}, bf16[2048,256]{1,0:T(8,128)(2,1)}, u32[]{:S(2)}) copy-start(bf16[2048,256]{1,0:T(8,128)(2,1)} %copy-done.10) | copy-start | bytes 3145732
  156.3 31.9 %all-to-all-start.3 = ((bf16[1,16,128,256]{3,1,0,2:T(8,128)(2,1)}), bf16[1,16,128,256]{3,1,0,2:T(8,128)(2,1)}, u32[]{:S(2)}, u32[]{:S(2)}) async-start(bf16[1,16,128,256]{3,1,0,2:T(8,128)(2,1)} %multiply_convert_fusion.1), calls=%async_computation.3 | async-start | bytes 2097152 | tf_op jit(solution)/shard_map/all_to_all | solution.py:132
  161.9 59.7 %copy-start.13 = (bf16[2048,256]{1,0:T(8,128)(2,1)S(1)}, bf16[2048,256]{1,0:T(8,128)(2,1)}, u32[]{:S(2)}) copy-start(bf16[2048,256]{1,0:T(8,128)(2,1)} %copy-done.12) | copy-start | bytes 3145732
  188.2 29.8 %all-to-all-start.1 = ((bf16[1,16,128,256]{3,1,0,2:T(8,128)(2,1)}), bf16[1,16,128,256]{3,1,0,2:T(8,128)(2,1)}, u32[]{:S(2)}, u32[]{:S(2)}) async-start(bf16[1,16,128,256]{3,1,0,2:T(8,128)(2,1)} %copy.173), calls=%async_computation.1 | async-start | bytes 2097152 | tf_op jit(solution)/shard_map/all_to_all | solution.py:131
  218.1 29.4 %all-to-all-start = ((bf16[1,16,128,256]{3,1,0,2:T(8,128)(2,1)}), bf16[1,16,128,256]{3,1,0,2:T(8,128)(2,1)S(1)}, u32[]{:S(2)}, u32[]{:S(2)}) async-start(bf16[1,16,128,256]{3,1,0,2:T(8,128)(2,1)} %copy.168), calls=%async_computation | async-start | bytes 2097152 | tf_op jit(solution)/shard_map/all_to_all | solution.py:129
  247.5 7.7 %copy-start.15 = (bf16[1,16,128,256]{3,1,0,2:T(8,128)(2,1)}, bf16[1,16,128,256]{3,1,0,2:T(8,128)(2,1)S(1)}, u32[]{:S(2)}) copy-start(bf16[1,16,128,256]{3,1,0,2:T(8,128)(2,1)S(1)} %all-to-all-done) | copy-start | bytes 3145732
  247.5 37.7 %all-to-all-start.2 = ((bf16[1,16,128,256]{3,1,0,2:T(8,128)(2,1)}), bf16[1,16,128,256]{3,1,0,2:T(8,128)(2,1)}, u32[]{:S(2)}, u32[]{:S(2)}) async-start(bf16[1,16,128,256]{3,1,0,2:T(8,128)(2,1)} %copy.180), calls=%async_computation.2 | async-start | bytes 2097152 | tf_op jit(solution)/shard_map/all_to_all | solution.py:130
  251.7 204.9 %all-reduce.2.cloned.1.call-start = ((), (), s32[]{:S(2)}) async-start(), calls=%async_computation.7 | async-start | bytes 9437184 | tf_op jit(solution)/shard_map/psum | solution.py:161
  271.2 2.0 copy-start.7
  271.2 7.0 %copy-start.16 = (bf16[1,16,128,256]{3,1,0,2:T(8,128)(2,1)S(1)}, bf16[1,16,128,256]{3,1,0,2:T(8,128)(2,1)}, u32[]{:S(2)}) copy-start(bf16[1,16,128,256]{3,1,0,2:T(8,128)(2,1)} %copy-done.15) | copy-start | bytes 3145732
  291.5 22.4 %copy-start.5 = (bf16[1,16,128,256]{2,3,1,0:T(8,128)(2,1)S(1)}, bf16[1,16,128,256]{2,3,1,0:T(8,128)(2,1)}, u32[]{:S(2)}) copy-start(bf16[1,16,128,256]{2,3,1,0:T(8,128)(2,1)} %copy.204) | copy-start | bytes 3145732
  325.5 2.6 copy-start.20
  364.4 102.8 %all-gather.6.cloned.1.call-start = ((), (), s32[]{:S(2)}) async-start(), calls=%async_computation.8 | async-start | bytes 2985984 | tf_op jit(solution)/shard_map/all_gather | solution.py:170
  365.0 110.5 %all-gather.8.cloned.1.call-start = ((), (), s32[]{:S(2)}) async-start(), calls=%async_computation.9 | async-start | bytes 2985984 | tf_op jit(solution)/shard_map/all_gather | solution.py:177
  365.6 174.9 %reduce-scatter.2.cloned.1.call-start = ((), (), s32[]{:S(2)}) async-start(), calls=%async_computation.10 | async-start | bytes 5898240 | tf_op jit(solution)/shard_map/reduce_scatter | solution.py:182
  461.9 2.1 copy-start.2
  461.9 2.1 copy-start.18
Sparse Core Ops, SparseCore 0:
  9.7 40.1 all-gather.3
  364.6 92.0 all-reduce.1
  494.0 46.4 reduce-scatter.1
Sparse Core Ops, SparseCore 1:
  367.1 52.9 all-gather.5
  422.1 53.4 all-gather.7
where the time goes:
time: 554 us; the launch traced here: 551 us
  waiting for transfers between devices  260 us (47%)
  local copies, waits for them, and re-layouts  89.8 us (16%)
  matrix products  89.8 us (16%)
  other arithmetic  47.2 us (9%)
  blocking collectives  30.6 us (6%)
  starting transfers between devices  17.9 us (3%)
  between operations  15.3 us (3%)
    psum x1, waiting for transfers between devices, shards(): lax.psum(partial_value.astype(jnp.bfloat16), 'mp').astype(jnp.float32)  91 us
    reduce_scatter x1, waiting for transfers between devices, shards(): lax.psum_scatter(downward.astype(jnp.bfloat16), 'mp', scatter_dimension=2...  46.6 us
    dot_general x2, matrix products, recurrence(): jnp.einsum('nhbqc,nhbsc->nhbqs', queries, weighted, precision=lax.Precisi...  44.5 us
    transpose x14, local copies, waits for them, and re-layouts, heads_first(): return shaped.transpose(0, 2, 1, 3)  42.1 us
    all_gather x1, waiting for transfers between devices, shards(): lax.all_gather(incoming_image_patches, 'mp', axis=2, tiled=True)  40.9 us
    all_to_all x1, blocking collectives, shards(): lax.all_to_all(back_grid, 'seq', split_axis=1, concat_axis=2, tiled=True)  30.6 us
    all_to_all x1, waiting for transfers between devices, shards(): lax.all_to_all(recept_grid, 'seq', split_axis=2, concat_axis=1, tiled=True)  24.2 us
    all_to_all x1, waiting for transfers between devices, shards(): lax.all_to_all(decay_grid, 'seq', split_axis=2, concat_axis=1, tiled=True)  24 us
  transfers between devices with their start and end apart: 9, of which 7 were waited for; matrix products, arithmetic and copies ran while one was open for 9% of the time, Pallas kernels for 0%

commit v1 on v0

v1 whole, which is shorter than its diff:
```python
import functools
import math

import jax
import jax.numpy as jnp
from jax import lax
from jax.experimental import pallas as pl
from jax.sharding import Mesh, PartitionSpec as P

SUBSPACE_SIZE = 64
MP = ("mx", "mc")


def layer_norm(inputs, gain):
    values = inputs.astype(jnp.float32)
    average = jnp.mean(values, axis=-1, keepdims=True)
    centred = values - average
    spread = jnp.mean(centred * centred, axis=-1, keepdims=True)
    return (centred * lax.rsqrt(spread + 1e-05) * gain).astype(jnp.bfloat16)


def split_dot(a, b):
    high = a.astype(jnp.bfloat16)
    low = (a - high.astype(jnp.float32)).astype(jnp.bfloat16)
    return jnp.dot(high, b, preferred_element_type=jnp.float32) + jnp.dot(
        low, b, preferred_element_type=jnp.float32
    )


def recurrence_kernel(
    lines, width, rkl_ref, v_ref, right_ref, base_ref, bonus_ref, gain_ref, tri_ref, same_ref, out_ref
):
    length = rkl_ref.shape[1]
    nheads = width // SUBSPACE_SIZE
    lane_head = lax.broadcasted_iota(jnp.int32, (1, width), 1) // SUBSPACE_SIZE
    earlier = lax.broadcasted_iota(jnp.int32, (length, length), 0) > lax.broadcasted_iota(
        jnp.int32, (length, length), 1
    )
    tri = tri_ref[...]
    same = same_ref[...]
    for line in range(lines):
        recept = rkl_ref[line, :, :width].astype(jnp.float32)
        keying = rkl_ref[line, :, width : 2 * width].astype(jnp.float32)
        latent = rkl_ref[line, :, 2 * width :]
        valued = v_ref[line]
        decay = (
            -0.7
            * jax.nn.sigmoid(
                base_ref[...] + jnp.dot(latent, right_ref[...], preferred_element_type=jnp.float32)
            )
        ).astype(jnp.bfloat16)
        running = jnp.dot(tri, decay, preferred_element_type=jnp.float32)
        middle = length // 2
        shifted = running - running[middle : middle + 1, :]
        queries = (recept * jnp.exp(shifted - decay.astype(jnp.float32))).astype(jnp.bfloat16)
        weighted = (keying * jnp.exp(-shifted)).astype(jnp.bfloat16)
        zero = jnp.zeros_like(queries)
        stacked = jnp.concatenate(
            [jnp.where(lane_head == head, queries, zero) for head in range(nheads)], axis=0
        )
        scores = lax.dot_general(
            stacked, weighted, (((1,), (1,)), ((), ())), preferred_element_type=jnp.float32
        )
        current = split_dot(recept * bonus_ref[...] * keying, same) * float(SUBSPACE_SIZE)
        summed = current * valued.astype(jnp.float32)
        for head in range(nheads):
            part = jnp.where(earlier, scores[head * length : (head + 1) * length], 0.0)
            product = jnp.dot(part.astype(jnp.bfloat16), valued, preferred_element_type=jnp.float32)
            summed = summed + jnp.where(lane_head == head, product, 0.0)
        centred = summed - split_dot(summed, same)
        spread = jnp.dot(
            (centred * centred).astype(jnp.bfloat16), same, preferred_element_type=jnp.float32
        )
        out_ref[line] = (centred * lax.rsqrt(spread + 0.00064) * gain_ref[...]).astype(jnp.bfloat16)


def recurrence(rkl, valued, right, base, bonus, gain, lines):
    number, length, width = valued.shape
    rank = right.shape[0]
    lines = math.gcd(lines, number)
    places = jnp.arange(length)
    tri = (places[:, None] >= places[None, :]).astype(jnp.bfloat16)
    heads = jnp.arange(width) // SUBSPACE_SIZE
    same = (heads[:, None] == heads[None, :]).astype(jnp.bfloat16) / SUBSPACE_SIZE
    fixed = lambda shape: pl.BlockSpec(shape, lambda i: (0, 0))
    wide = rkl.shape[2]
    return pl.pallas_call(
        functools.partial(recurrence_kernel, lines, width),
        grid=(number // lines,),
        in_specs=[
            pl.BlockSpec((lines, length, wide), lambda i: (i, 0, 0)),
            pl.BlockSpec((lines, length, width), lambda i: (i, 0, 0)),
            fixed((rank, width)),
            fixed((1, width)),
            fixed((1, width)),
            fixed((1, width)),
            fixed((length, length)),
            fixed((width, width)),
        ],
        out_specs=pl.BlockSpec((lines, length, width), lambda i: (i, 0, 0)),
        out_shape=jax.ShapeDtypeStruct((number, length, width), jnp.bfloat16),
        cost_estimate=pl.CostEstimate(
            flops=number * length * width * 4 * (length * 6 + width * 4),
            bytes_accessed=number * length * (wide + 2 * width) * 2,
            transcendentals=number * length * width * 3,
        ),
    )(rkl, valued, right, base[None], bonus[None], gain[None], tri, same)


def gather_columns(own):
    if lax.axis_size("mx") != 2 or lax.axis_size("mc") != 2:
        return lax.all_gather(own, MP, axis=2, tiled=True)
    swap = [(0, 1), (1, 0)]
    across = lax.ppermute(own, "mx", swap)
    beside = lax.ppermute(own, "mc", swap)
    corner = lax.ppermute(across, "mc", swap)
    first = lax.axis_index("mx") == 0
    left_core = lax.axis_index("mc") == 0
    near = (jnp.where(left_core, own, beside), jnp.where(left_core, beside, own))
    far = (jnp.where(left_core, across, corner), jnp.where(left_core, corner, across))
    return jnp.concatenate(
        [jnp.where(first, a, b) for a, b in zip(near, far)]
        + [jnp.where(first, b, a) for a, b in zip(near, far)],
        axis=2,
    )


def shards(
    incoming,
    first_gain,
    acceptance,
    addressing,
    content,
    left,
    right,
    baseline,
    reward,
    row_gain,
    col_gain,
    projection,
    later_gain,
    mix_in,
    mix_out,
):
    images, rows, _, model_width = incoming.shape
    width = acceptance.shape[1]
    halves = jnp.concatenate([mix_in, mix_out.T], axis=0)
    depth = mix_in.shape[0]
    if SPLIT == 1:
        halves = lax.all_gather(halves, "mx", axis=1, tiled=True)
    halves = lax.all_gather(halves, "seq", axis=0, tiled=False)
    if SPLIT == 2:
        halves = lax.all_gather(halves, "mx", axis=2, tiled=True)
    whole_in = halves[:, :depth].reshape(-1, halves.shape[2])
    whole_out = halves[:, depth:].reshape(-1, halves.shape[2])
    whole_projection = lax.all_gather(projection, MP, axis=0, tiled=True)
    xn1 = gather_columns(layer_norm(incoming, first_gain))
    cols = xn1.shape[2]
    tokens = xn1.reshape(-1, model_width)
    rk = jnp.dot(
        tokens, jnp.concatenate([acceptance, addressing], axis=1), preferred_element_type=jnp.float32
    ).astype(jnp.bfloat16)
    latent = jnp.tanh(jnp.dot(tokens, left, preferred_element_type=jnp.float32)).astype(jnp.bfloat16)
    valued = jnp.dot(tokens, content, preferred_element_type=jnp.float32).astype(jnp.bfloat16)
    rkl = jnp.concatenate([rk, latent], axis=1)
    wide = rkl.shape[1]

    def by_columns(array):
        last = array.shape[-1]
        turned = jnp.swapaxes(array.reshape(images, rows, cols, last), 1, 2)
        moved = lax.all_to_all(turned, "seq", split_axis=1, concat_axis=2, tiled=True)
        return moved.reshape(-1, moved.shape[2], last)

    col_rkl = by_columns(rkl)
    row_out = recurrence(
        rkl.reshape(-1, cols, wide),
        valued.reshape(-1, cols, width),
        right,
        baseline,
        reward,
        row_gain,
        2,
    )
    col_valued = by_columns(row_out)
    col_out = recurrence(col_rkl, col_valued, right, baseline, reward, col_gain, 2)
    own_cols = col_out.shape[0] // images
    col_out = col_out.reshape(images, own_cols, -1, width)
    back = lax.all_to_all(col_out, "seq", split_axis=2, concat_axis=1, tiled=True)
    mine = lax.all_to_all(back, MP, split_axis=1, concat_axis=3, tiled=True)
    mine = jnp.swapaxes(mine, 1, 2)
    attended = jnp.dot(
        mine.reshape(-1, mine.shape[3]), whole_projection, preferred_element_type=jnp.float32
    ).reshape(incoming.shape)
    residual = (incoming.astype(jnp.float32) + attended).astype(jnp.bfloat16)
    xn2 = layer_norm(residual, later_gain).reshape(-1, model_width)
    share = "mc" if SPLIT else MP
    xn2 = lax.all_gather(xn2, share, axis=0, tiled=True)
    positive = jnp.maximum(jnp.dot(xn2, whole_in, preferred_element_type=jnp.float32), 0.0)
    hidden = (positive * positive).astype(jnp.bfloat16)
    downward = lax.dot_general(
        hidden, whole_out, (((1,), (1,)), ((), ())), preferred_element_type=jnp.float32
    ).astype(jnp.bfloat16)
    mixed = lax.psum_scatter(downward, share, scatter_dimension=0, tiled=True)
    return (
        residual.astype(jnp.float32) + mixed.astype(jnp.float32).reshape(residual.shape)
    ).astype(jnp.bfloat16)


SPLIT = 2


def solution(mesh):
    seq, mp = mesh.devices.shape
    cores = math.gcd(mp, 2)
    fine = Mesh(mesh.devices.reshape(seq, mp // cores, cores), ("seq", "mx", "mc"))
    placed = (
        P(None, "seq", MP, None),
        P(),
        P(None, MP),
        P(None, MP),
        P(None, MP),
        P(),
        P(None, MP),
        P(MP),
        P(MP),
        P(MP),
        P(MP),
        P(MP, None),
        P(),
        P("seq", MP),
        P(MP, "seq"),
    )
    return jax.shard_map(
        shards, mesh=fine, in_specs=placed, out_specs=P(None, "seq", MP, None), check_vma=False
    )
```

time: 554 us -> 339 us (0.61)
  waiting for transfers between devices: 260 us -> 148 us
  matrix products: 89.8 us -> 31.9 us
  local copies, waits for them, and re-layouts: 89.8 us -> 35.4 us
  Pallas kernels: 0 us -> 35.5 us
  other arithmetic: 47.2 us -> 15.4 us
  blocking collectives: 30.6 us -> 46.3 us
  starting transfers between devices: 17.9 us -> 11.6 us
    psum x1 -> x0, waiting for transfers between devices: 91 us -> none  [shards(): lax.psum(partial_value.astype(jnp.bfloat16), 'mp').astype(jnp.float32)]
    dot_general x10 -> x5, matrix products: 89.8 us -> 31.9 us  [the longest x1 18.7 us: shards(): lax.dot_general(hidden, whole_out, (((1,), (1,)), ((), ())), preferred_el...]
    transpose x15 -> x1, local copies, waits for them, and re-layouts: 43.8 us -> 2.78 us  [by_columns(): turned = jnp.swapaxes(array.reshape(images, rows, cols, last), 1, 2)]
    pallas_call x0 -> x2, Pallas kernels: none -> 35.5 us  [recurrence(): pl.pallas_call(functools.partial(recurrence_kernel, lines, width), grid=(...]
    reduce_scatter x1, waiting for transfers between devices: 46.6 us -> 11.4 us  [shards(): mixed = lax.psum_scatter(downward, share, scatter_dimension=0, tiled=True)]
    ppermute x0 -> x3, waiting for transfers between devices: none -> 27.8 us  [the longest x1 26.1 us: gather_columns(): across = lax.ppermute(own, 'mx', swap)]
    all_to_all x1 -> x2, blocking collectives: 30.6 us -> 46.3 us  [the longest x1 29.3 us: shards(): lax.all_to_all(col_out, 'seq', split_axis=2, concat_axis=1, tiled=True)]
    another operation x3 -> x0, other arithmetic: 14.1 us -> none  [the longest x2 14.1 us: recurrence(): running = jnp.cumsum(decays, axis=2)]
  transfers between devices with their start and end apart: 9 -> 10, of which waited for: 7 -> 6; matrix products, arithmetic and copies ran while one was open for 9% -> 17% of each run, Pallas kernels for 0% -> 11%
where the time goes in v1:
time: 339 us; the launch traced here: 338 us
  waiting for transfers between devices  148 us (44%)
  blocking collectives  46.3 us (14%)
  Pallas kernels  35.5 us (10%)
  local copies, waits for them, and re-layouts  35.4 us (10%)
  matrix products  31.9 us (9%)
  other arithmetic  15.4 us (5%)
  between operations  13.3 us (4%)
  starting transfers between devices  11.6 us (3%)
    all_to_all x2, waiting for transfers between devices, by_columns(): lax.all_to_all(turned, 'seq', split_axis=1, concat_axis=2, tiled=True)  73.4 us
    all_gather x1, waiting for transfers between devices, shards(): halves = lax.all_gather(halves, 'seq', axis=0, tiled=False)  35.7 us
    pallas_call x2, Pallas kernels, recurrence(): pl.pallas_call(functools.partial(recurrence_kernel, lines, width), grid=(...  35.5 us
    all_to_all x1, blocking collectives, shards(): lax.all_to_all(col_out, 'seq', split_axis=2, concat_axis=1, tiled=True)  29.3 us
    ppermute x1, waiting for transfers between devices, gather_columns(): across = lax.ppermute(own, 'mx', swap)  26.1 us
    dot_general x1, matrix products, shards(): lax.dot_general(hidden, whole_out, (((1,), (1,)), ((), ())), preferred_el...  18.7 us
    all_to_all x1, blocking collectives, shards(): mine = lax.all_to_all(back, MP, split_axis=1, concat_axis=3, tiled=True)  17 us
    reduce_scatter x1, waiting for transfers between devices, shards(): mixed = lax.psum_scatter(downward, share, scatter_dimension=0, tiled=True)  11.4 us
  transfers between devices with their start and end apart: 10, of which 6 were waited for; matrix products, arithmetic and copies ran while one was open for 17% of the time, Pallas kernels for 11%

profile of v1, /device:TPU:0, one launch (start us, length us, event | category | flops | bytes accessed | tf_op | source)
XLA Modules:
  0.0 337.8 jit_solution(9941716943077430242)
XLA Ops:
  6.5 2.2 pad_maximum_fusion.2
  8.8 0.0 all-gather.6.cloned.1.call-start
  8.8 0.2 convert_reduce_fusion.1
  9.1 0.5 fusion.8
  9.5 0.4 fusion.10
  10.0 3.0 collective-permute-start.1
  13.0 26.1 %collective-permute-done.1 = bf16[1,16,32,1152]{3,2,1,0:T(8,128)(2,1)} collective-permute-done((bf16[1,16,32,1152]{3,2,1,0:T(8,128)(2,1)S(1)}, bf16[1,16,32,1152]{3,2,1,0:T(8,128)(2,1)}, u32[]{:S(2)}, u32[]{:S(2)}) %collective-permute-start.1) | collective-permute-done | bytes 1179680 | tf_op jit(solution)/shard_map/ppermute | solution.py:114
  39.2 0.8 compare_select_fusion.same_ref
  39.9 0.6 fusion.18.tri_ref
  40.6 1.7 collective-permute-done.2
  42.3 2.5 broadcast_select_fusion.7
  44.8 0.7 pad_maximum_fusion
  45.5 0.2 copy-done.4
  45.7 1.6 fusion.13
  47.3 0.4 copy-done.2
  47.7 0.1 copy-done.8
  47.9 3.2 convolution_convert_fusion.1
  51.0 3.0 pad_maximum_fusion.1
  54.1 4.4 %copy.34 = bf16[2048,576]{1,0:T(8,128)(2,1)} copy(bf16[2048,576]{0,1:T(8,128)(2,1)} %get-tuple-element.11) | data formatting | bytes 4718592 | tf_op jit(solution)/shard_map/concatenate | solution.py:165
  58.4 4.8 %convolution_convert_fusion.2 = bf16[2048,256]{1,0:T(8,128)(2,1)} fusion(bf16[2048,1152]{1,0:T(8,128)(2,1)} %bitcast.72, bf16[1152,256]{1,0:T(8,128)(2,1)S(1)} %copy-done), kind=kOutput, calls=%fused_computation.16 | convolution fusion | flops 1208483840 | bytes 6356992 | tf_op jit(solution)/shard_map/dot_general | solution.py:164
  63.3 35.7 %all-gather.12.cloned.1.call-done = bf16[2304,1152]{1,0:T(8,128)(2,1)} async-done(((bf16[288,1152]{1,0:T(8,128)(2,1)}), bf16[2304,1152]{1,0:T(8,128)(2,1)}) %all-gather.12.cloned.1.call-update) | async-done | bytes 5308432 | tf_op jit(solution)/shard_map/all_gather | solution.py:151
  99.0 17.8 %shard_map.145 = bf16[16,128,256]{2,1,0:T(8,128)(2,1)} custom-call(bf16[16,128,576]{2,1,0:T(8,128)(2,1)} %bitcast.83, bf16[16,128,256]{2,1,0:T(8,128)(2,1)} %bitcast.96, bf16[64,256]{1,0:T(8,128)(2,1)} %right_ref.3, f32[1,256]{1,0:T(1,128)} %bitcast.91, f32[1,256]{1,0:T(1,128)} %bitcast.93, f32[1,256]{1,0:T(1,128)} %bitcast.90, ...), custom_call_target="tpu_custom_call" | custom-call | flops 3758096384 | bytes 4456448 | tf_op jit(solution)/shard_map/pallas_call | solution.py:87
  116.8 2.8 copy.35
  119.5 3.6 %all-to-all-start.1 = ((bf16[1,128,16,256]{3,2,0,1:T(8,128)(2,1)}), bf16[1,128,16,256]{3,2,0,1:T(8,128)(2,1)S(1)}, u32[]{:S(2)}, u32[]{:S(2)}) async-start(bf16[1,128,16,256]{3,2,0,1:T(8,128)(2,1)} %copy.35), calls=%async_computation.1 | async-start | bytes 2097152 | tf_op jit(solution)/shard_map/all_to_all | solution.py:171
  123.1 3.9 %copy.42 = bf16[72,8,16,128]{3,2,1,0:T(8,128)(2,1)} copy(bf16[72,8,16,128]{3,1,2,0:T(8,128)(2,1)} %get-tuple-element.12) | data formatting | bytes 4718592
  127.0 5.4 %copy.32 = bf16[1,16,128,576]{3,1,0,2:T(8,128)(2,1)} copy(bf16[1,16,128,576]{2,1,3,0:T(8,128)(2,1)} %bitcast.74) | data formatting | bytes 4718592 | tf_op jit(solution)/shard_map/reshape | solution.py:170
  132.4 16.0 %all-to-all-done.1 = bf16[1,128,16,256]{3,2,0,1:T(8,128)(2,1)S(1)} async-done(((bf16[1,128,16,256]{3,2,0,1:T(8,128)(2,1)}), bf16[1,128,16,256]{3,2,0,1:T(8,128)(2,1)S(1)}, u32[]{:S(2)}, u32[]{:S(2)}) %all-to-all-start.1) | async-done | bytes 1048608 | tf_op jit(solution)/shard_map/all_to_all | solution.py:171
  148.4 4.4 %all-to-all-start = ((bf16[1,128,16,576]{3,2,0,1:T(8,128)(2,1)}), bf16[1,128,16,576]{3,2,0,1:T(8,128)(2,1)}, u32[]{:S(2)}, u32[]{:S(2)}) async-start(bf16[1,128,16,576]{3,2,0,1:T(8,128)(2,1)} %bitcast.73), calls=%async_computation | async-start | bytes 5242880 | tf_op jit(solution)/shard_map/all_to_all | solution.py:171
  152.8 0.2 all-gather.8.cloned.1.call-start
  153.0 1.1 copy.36
  154.1 57.4 %all-to-all-done = bf16[1,128,16,576]{3,2,0,1:T(8,128)(2,1)} async-done(((bf16[1,128,16,576]{3,2,0,1:T(8,128)(2,1)}), bf16[1,128,16,576]{3,2,0,1:T(8,128)(2,1)}, u32[]{:S(2)}, u32[]{:S(2)}) %all-to-all-start) | async-done | bytes 2359328 | tf_op jit(solution)/shard_map/all_to_all | solution.py:171
  211.5 3.6 %copy.33 = bf16[1,16,8,16,576]{4,3,2,1,0:T(8,128)(2,1)} copy(bf16[1,16,8,16,576]{4,3,1,2,0:T(8,128)(2,1)} %bitcast.3) | data formatting | bytes 4718592 | tf_op jit(solution)/shard_map/all_to_all | solution.py:171
  215.1 17.8 %shard_map.146 = bf16[16,128,256]{2,1,0:T(8,128)(2,1)} custom-call(bf16[16,128,576]{2,1,0:T(8,128)(2,1)} %bitcast.84, bf16[16,128,256]{2,1,0:T(8,128)(2,1)} %bitcast.86, bf16[64,256]{1,0:T(8,128)(2,1)} %right_ref.3, f32[1,256]{1,0:T(1,128)} %bitcast.92, f32[1,256]{1,0:T(1,128)} %bitcast.94, f32[1,256]{1,0:T(1,128)} %bitcast.95, ...), custom_call_target="tpu_custom_call" | custom-call | flops 3758096384 | bytes 4456448 | tf_op jit(solution)/shard_map/pallas_call | solution.py:87
  232.8 1.8 copy.37
  234.6 29.3 %all_to_all.66 = bf16[1,16,128,256]{3,1,0,2:T(8,128)(2,1)S(1)} all-to-all(bf16[1,16,128,256]{3,1,0,2:T(8,128)(2,1)S(1)} %copy.37), channel_id=1, replica_groups=mesh['seq'=8,'mx'=2,'mc'=2] {'seq'}, dimensions={2} | all-to-all | bytes 2097152 | tf_op jit(solution)/shard_map/all_to_all | solution.py:188
  264.0 0.3 copy.38
  264.3 0.1 copy.39
  264.4 17.0 %all_to_all.67 = bf16[1,128,16,256]{3,2,0,1:T(8,128)(2,1)S(1)} all-to-all(bf16[1,128,16,256]{3,2,0,1:T(8,128)(2,1)S(1)} %bitcast.81), channel_id=1, replica_groups=mesh['seq'=8,'mx'=2,'mc'=2] {'mx','mc'}, dimensions={1} | all-to-all | bytes 2097152 | tf_op jit(solution)/shard_map/all_to_all | solution.py:189
  281.4 0.8 copy.41
  282.2 1.5 all_to_all.61
  283.7 3.6 %convert_reduce_fusion = (f32[16,32]{1,0:T(8,128)S(1)}, bf16[1,16,32,1152]{3,2,1,0:T(8,128)(2,1)S(1)}) fusion(bf16[1024,1152]{1,0:T(8,128)(2,1)} %all-gather.6.cloned.1.call-done, bf16[1,32,16,1024]{3,1,2,0:T(8,128)(2,1)} %all_to_all.61, bf16[1,16,32,1152]{3,2,1,0:T(8,128)(2,1)S(1)} %copy-done.3), kind=kOutput, calls=%fused_computation.5 | convolution fusion | flops 1210908160 | bytes 5769216 | tf_op jit(solution)/shard_map/dot_general | solution.py:191
  287.3 0.5 fusion.5
  287.8 1.4 fusion.7
  289.3 0.3 reduce-scatter.2.cloned.1.call-start
  289.6 9.0 %fusion.22 = (bf16[8,144,2304]{2,1,0:T(8,128)(2,1)}, bf16[8,144,2304]{2,1,0:T(8,128)(2,1)}) fusion(bf16[8,288,2304]{2,1,0:T(8,128)(2,1)} %all-gather.10.cloned.1.call-done), kind=kLoop, calls=%fused_computation.55 | loop fusion | bytes 21233664 | tf_op jit(solution)/shard_map/slice | solution.py:154
  298.6 18.7 %convolution_convert_fusion = bf16[1024,1152]{1,0:T(8,128)(2,1)} fusion(bf16[1152,2304]{1,0:T(8,128)(2,1)} %bitcast.77, bf16[1024,1152]{1,0:T(8,128)(2,1)} %all-gather.8.cloned.1.call-done, bf16[1152,2304]{1,0:T(8,128)(2,1)} %bitcast.76), kind=kOutput, calls=%fused_computation.2 | convolution fusion | flops 10879893504 | bytes 15335424 | tf_op jit(solution)/shard_map/dot_general | solution.py:200
  317.3 11.4 %reduce-scatter.2.cloned.1.call-done = bf16[512,1152]{1,0:T(8,128)(2,1)} async-done(((bf16[1024,1152]{1,0:T(8,128)(2,1)}), bf16[512,1152]{1,0:T(8,128)(2,1)}) %reduce-scatter.2.cloned.1.call-update) | async-done | bytes 1179664 | tf_op jit(solution)/shard_map/reduce_scatter | solution.py:203
  328.7 2.6 fusion.11
  (33 shorter events, 0.2 us)
Async XLA Ops:
  6.5 51.9 %copy-start = (bf16[1152,256]{1,0:T(8,128)(2,1)S(1)}, bf16[1152,256]{1,0:T(8,128)(2,1)}, u32[]{:S(2)}) copy-start(bf16[1152,256]{1,0:T(8,128)(2,1)} %param.19) | copy-start | bytes 1769476
  6.5 2.3 copy-start.3
  6.5 3.0 copy-start.5
  6.5 92.4 %all-gather.12.cloned.1.call-start = ((), (), s32[]{:S(2)}) async-start(), calls=%async_computation.9 | async-start | bytes 5971968 | tf_op jit(solution)/shard_map/all_gather | solution.py:151
  8.8 275.0 %all-gather.6.cloned.1.call-start = ((), (), s32[]{:S(2)}) async-start(), calls=%async_computation.5 | async-start | bytes 2949120 | tf_op jit(solution)/shard_map/all_gather | solution.py:156
  10.0 29.1 %collective-permute-start.1 = (bf16[1,16,32,1152]{3,2,1,0:T(8,128)(2,1)S(1)}, bf16[1,16,32,1152]{3,2,1,0:T(8,128)(2,1)}, u32[]{:S(2)}, u32[]{:S(2)}) collective-permute-start(bf16[1,16,32,1152]{3,2,1,0:T(8,128)(2,1)S(1)} %fusion.10), channel_id=1, source_target_pairs={{0,2},{2,0},{1,3},{3,1},{4,6},{6,4},{5,7},{7,5},{8,10},{10,8},{9,1... | collective-permute-start | bytes 3538952 | tf_op jit(solution)/shard_map/ppermute | solution.py:114
  13.0 27.6 %collective-permute-start = (bf16[1,16,32,1152]{3,2,1,0:T(8,128)(2,1)S(1)}, bf16[1,16,32,1152]{3,2,1,0:T(8,128)(2,1)}, u32[]{:S(2)}, u32[]{:S(2)}) collective-permute-start(bf16[1,16,32,1152]{3,2,1,0:T(8,128)(2,1)S(1)} %fusion.10), channel_id=1, source_target_pairs={{0,1},{1,0},{2,3},{3,2},{4,5},{5,4},{6,7},{7,6},{8,9},{9,8},{10,11... | collective-permute-start | bytes 3538952 | tf_op jit(solution)/shard_map/ppermute | solution.py:115
  39.1 3.2 collective-permute-start.2
  39.1 250.5 %all-gather.10.cloned.1.call-start = ((), (), s32[]{:S(2)}) async-start(), calls=%async_computation.7 | async-start | bytes 15925248 | tf_op jit(solution)/shard_map/all_gather | solution.py:153
  44.8 0.9 copy-start.4
  45.5 2.2 copy-start.2
  45.7 2.0 copy-start.7
  45.7 2.1 copy-start.8
  119.5 28.8 %all-to-all-start.1 = ((bf16[1,128,16,256]{3,2,0,1:T(8,128)(2,1)}), bf16[1,128,16,256]{3,2,0,1:T(8,128)(2,1)S(1)}, u32[]{:S(2)}, u32[]{:S(2)}) async-start(bf16[1,128,16,256]{3,2,0,1:T(8,128)(2,1)} %copy.35), calls=%async_computation.1 | async-start | bytes 2097152 | tf_op jit(solution)/shard_map/all_to_all | solution.py:171
  148.4 63.1 %all-to-all-start = ((bf16[1,128,16,576]{3,2,0,1:T(8,128)(2,1)}), bf16[1,128,16,576]{3,2,0,1:T(8,128)(2,1)}, u32[]{:S(2)}, u32[]{:S(2)}) async-start(bf16[1,128,16,576]{3,2,0,1:T(8,128)(2,1)} %bitcast.73), calls=%async_computation | async-start | bytes 5242880 | tf_op jit(solution)/shard_map/all_to_all | solution.py:171
  152.8 145.8 %all-gather.8.cloned.1.call-start = ((), (), s32[]{:S(2)}) async-start(), calls=%async_computation.6 | async-start | bytes 3538944 | tf_op jit(solution)/shard_map/all_gather | solution.py:197
  283.7 4.1 %copy-start.6 = (f32[1152]{0:T(1024)S(1)}, f32[1152]{0:T(1024)}, u32[]{:S(2)}) copy-start(f32[1152]{0:T(1024)} %param.27) | copy-start | bytes 13828
  289.3 39.4 %reduce-scatter.2.cloned.1.call-start = ((), (), s32[]{:S(2)}) async-start(), calls=%async_computation.8 | async-start | bytes 3538944 | tf_op jit(solution)/shard_map/reduce_scatter | solution.py:203
  317.3 13.9 %copy-start.1 = (bf16[1152,256]{1,0:T(8,128)(2,1)S(1)}, bf16[1152,256]{1,0:T(8,128)(2,1)}, u32[]{:S(2)}) copy-start(bf16[1152,256]{1,0:T(8,128)(2,1)} %param.19) | copy-start | bytes 1769476
Sparse Core Ops, SparseCore 0:
  9.5 89.3 all-gather.11
  100.5 22.2 all-gather.5
  124.4 130.8 all-gather.9
  289.4 9.0 all-gather.7
  317.4 11.2 reduce-scatter.1
